TPU v7x, 32 devices: a whole 2x2x4 slice. The times are simulated.
32 devices in a mesh: dp: 16 (over z, y, x), fsdp: 2 (over core).
Axes of the slice: x: 2, y: 2, z: 4, core: 2. Of those that a mesh axis runs over, the one named last changes fastest.
Arguments:
- patches: bfloat16 [1024, 32, 1024], P(('dp', 'fsdp')), may hold values from -6 to 6
- rows: int32 [1024, 32], P(('dp', 'fsdp')), may hold values from 0 to 63
- cols: int32 [1024, 32], P(('dp', 'fsdp')), may hold values from 0 to 63
- keep: int32 [1024, 32], P(('dp', 'fsdp')), may hold values from 0 to 1, as said below
- images: int32 [1024, 32], P(('dp', 'fsdp')), may hold values from 0 to 3, never falling along the last dimension, each value on 1 to 16 neighbouring positions
- destination: int32 [2, 16, 32], P('fsdp'), may hold values from 0 to 15, as said below
- row_table: bfloat16 [64, 1024], replicated, may hold values from -6 to 6
- col_table: bfloat16 [64, 1024], replicated, may hold values from -6 to 6
- w_qkv: bfloat16 [1024, 3072], P('fsdp'), may hold values from -1 to 1
- w_out: bfloat16 [1024, 1024], P('fsdp'), may hold values from -0.1875 to 0.1875
- w_up: bfloat16 [1024, 4096], P('fsdp'), may hold values from -0.1875 to 0.1875
- w_down: bfloat16 [4096, 1024], P('fsdp'), may hold values from -0.09375 to 0.09375
Outputs:
- encoded: bfloat16 [1024, 32, 1024], P(('dp', 'fsdp'))
Inputs may be any that keep to these rules, and one draw needn't show every extreme that they name: keep is 0 or 1; the share of kept tokens differs from sequence to sequence. `destination`: for each fsdp index, every dp index is named by exactly 32 entries of the table, and no row names one dp index more than 2 times.
All inputs are finite; a program needn't handle non-finite values.
Results may differ from a plain program's by a relative error of at most 0.0065.
Values may be sent and summed in bfloat16 or wider, within the bound.
A program may use at most 192 MiB of HBM per device.

v0:
```python
import jax
import jax.numpy as jnp
from jax import lax
from jax.sharding import PartitionSpec as P

HEADS = 16
HEAD_DIM = 64


EPS = 1e-06


def layer_norm(values):
    center = values - jnp.mean(values, axis=-1, keepdims=True)
    spread = jnp.mean(center * center, axis=-1, keepdims=True)
    return center * lax.rsqrt(spread + EPS)


def attend(qkv, label, count, seq):
    parts = qkv.reshape(count, seq, 3, HEADS, HEAD_DIM)
    scores = jnp.einsum(
        "nqhd,nkhd->nhqk", parts[:, :, 0], parts[:, :, 1], preferred_element_type=jnp.float32
    ) * HEAD_DIM ** (-0.5)
    allowed = (label[:, :, None] == label[:, None, :]) & (label[:, None, :] > 0)
    allowed = allowed[:, None]
    scores = jnp.where(allowed, scores, -1e30)
    peak = jnp.max(scores, axis=-1, keepdims=True)
    weights = jnp.where(allowed, jnp.exp(scores - peak), 0.0)
    dropped = (label == 0).astype(jnp.float32)[:, None, :, None]
    total = jnp.sum(weights, axis=-1, keepdims=True) + dropped
    probs = (weights / total).astype(jnp.bfloat16)
    attended = jnp.einsum(
        "nhqk,nkhd->nqhd", probs, parts[:, :, 2], preferred_element_type=jnp.float32
    )
    return attended.astype(jnp.bfloat16).reshape(count * seq, HEADS * HEAD_DIM)


def local(
    patches, rows, cols, keep, images, destination, row_table, col_table, w_qkv, w_out, w_up, w_down
):
    blk, seq, width = patches.shape
    peers = lax.axis_size("dp")
    myself = lax.axis_index("dp")
    capacity = (blk + peers - 1) // peers
    full = (
        lax.all_gather(w_qkv, "fsdp", axis=0, tiled=True),
        lax.all_gather(w_out, "fsdp", axis=0, tiled=True),
        lax.all_gather(w_up, "fsdp", axis=0, tiled=True),
        lax.all_gather(w_down, "fsdp", axis=0, tiled=True),
    )
    grid = row_table.shape[0]
    slots = jnp.arange(grid, dtype=jnp.int32)
    onehot = jnp.concatenate(
        [
            (rows[..., None] == slots).astype(jnp.bfloat16),
            (cols[..., None] == slots).astype(jnp.bfloat16),
        ],
        axis=-1,
    )
    tables = jnp.concatenate([row_table, col_table], axis=0)
    places = jnp.einsum("nsg,gd->nsd", onehot, tables, preferred_element_type=jnp.float32)
    embedded = (patches.astype(jnp.float32) + places).astype(jnp.bfloat16)
    labels = keep * (images + 1)
    table = destination[0]
    mine = lax.dynamic_index_in_dim(table, myself, 0, keepdims=False)
    positions = jnp.arange(blk, dtype=jnp.int32)
    earlier = positions[:, None] > positions[None, :]
    same = mine[:, None] == mine[None, :]
    rank = jnp.sum((same & earlier).astype(jnp.int32), axis=1)
    sending_slot = mine * capacity + rank
    counts = jnp.sum((table == myself).astype(jnp.int32), axis=1)
    arrival = jnp.arange(peers * capacity, dtype=jnp.int32)
    filled = arrival % capacity < jnp.repeat(counts, capacity)
    order = jnp.argsort(jnp.where(filled, arrival, arrival + peers * capacity))[:blk]
    outgoing = (
        jnp.zeros((peers * capacity, seq, width), jnp.bfloat16).at[sending_slot].set(embedded)
    )
    outgoing_labels = (
        jnp.zeros((peers * capacity, seq), jnp.bfloat16)
        .at[sending_slot]
        .set(labels.astype(jnp.bfloat16))
    )
    arrived, arrived_labels = (
        lax.all_to_all(outgoing, "dp", split_axis=0, concat_axis=0, tiled=True),
        lax.all_to_all(outgoing_labels, "dp", split_axis=0, concat_axis=0, tiled=True),
    )
    blocks = jnp.take(arrived, order, axis=0)
    label = jnp.take(arrived_labels, order, axis=0).astype(jnp.float32)
    count = blocks.shape[0]
    inputs = blocks.astype(jnp.float32).reshape(count * seq, width)
    normed = layer_norm(inputs).astype(jnp.bfloat16)
    qkv = jnp.dot(normed, full[0], preferred_element_type=jnp.float32)
    attended = attend(qkv.astype(jnp.bfloat16), label, count, seq)
    projected = jnp.dot(attended, full[1], preferred_element_type=jnp.float32)
    mid = inputs + projected
    second = layer_norm(mid).astype(jnp.bfloat16)
    upper = jnp.dot(second, full[2], preferred_element_type=jnp.float32)
    activated = jax.nn.gelu(upper, approximate=True).astype(jnp.bfloat16)
    lowered = jnp.dot(activated, full[3], preferred_element_type=jnp.float32)
    result = mid + lowered
    live = label.reshape(count * seq, 1) > 0
    return jnp.where(live, result, 0.0).astype(jnp.bfloat16).reshape(count, seq, width)


def solution(mesh):
    in_specs = (
        P(("dp", "fsdp"), None, None),
        P(("dp", "fsdp"), None),
        P(("dp", "fsdp"), None),
        P(("dp", "fsdp"), None),
        P(("dp", "fsdp"), None),
        P("fsdp", None, None),
        P(),
        P(),
        P("fsdp", None),
        P("fsdp", None),
        P("fsdp", None),
        P("fsdp", None),
    )
    out_specs = P(("dp", "fsdp"), None, None)
    return jax.shard_map(local, mesh=mesh, in_specs=in_specs, out_specs=out_specs, check_vma=False)
```

profile of v0, /device:TPU:12, one launch (start us, length us, event | category | flops | bytes accessed | tf_op | source)
XLA Modules:
  0.0 187.0 jit_solution(17494195881643744161)
XLA Ops:
  6.6 0.7 all-gather.5.cloned.1.call-update
  7.3 0.0 all-gather.7.cloned.1.call-start
  7.3 0.7 all-gather.7.cloned.1.call-update
  8.0 0.0 all-gather.11.cloned.1.call-start
  8.1 0.7 all-gather.11.cloned.1.call-update
  8.8 0.2 convert_reduce_fusion.1
  9.0 1.2 scatter_custom_fusion
  10.2 7.2 %all-to-all-start = ((bf16[16,2,32]{2,1,0:T(2,128)(2,1)}), bf16[16,2,32]{2,1,0:T(2,128)(2,1)S(1)}, u32[]{:S(2)}, u32[]{:S(2)}) async-start(bf16[16,2,32]{2,1,0:T(2,128)(2,1)} %bitcast.4), calls=%async_computation | async-start | bytes 16384 | tf_op jit(solution)/shard_map/all_to_all | solution.py:85
  17.4 0.3 iota_compare_fusion
  17.8 2.7 %add_convert_fusion = bf16[32,32,1024]{2,1,0:T(8,128)(2,1)S(1)} fusion(bf16[32,32,1024]{2,1,0:T(8,128)(2,1)} %param.12, pred[32,32,64]{2,1,0:T(32,128)(4,1)S(1)} %get-tuple-element.16, pred[32,32,64]{2,1,0:T(32,128)(4,1)S(1)} %get-tuple-element.17, bf16[64,1024]{1,0:T(8,128)(2,1)S(1)} %copy-done.1, bf16[64,1024]{1,0:T(8,128)(2,1)S(1)} %copy-done.2), kind=kOutput, calls=%fused_computation.40 | convolution fusion | flops 272236544 | bytes 4587520 | tf_op jit(solution)/shard_map/nsg,gd->nsd/dot_general | solution.py:61
  20.5 1.6 broadcast_in_dim.98
  22.1 5.7 %scatter_fusion = bf16[32,32,1024]{2,1,0:T(8,128)(2,1)} fusion(bf16[32,32,1024]{2,1,0:T(8,128)(2,1)} %broadcast_in_dim.98, s32[32]{0:T(128)S(1)} %fusion.41, bf16[32,32,1024]{2,1,0:T(8,128)(2,1)S(1)} %add_convert_fusion), kind=kCustom, calls=%fused_computation.3 | custom fusion | bytes 6291584 | tf_op jit(solution)/shard_map/scatter | solution.py:76
  27.8 6.9 %all-to-all-start.1 = ((bf16[32,32,1024]{2,1,0:T(8,128)(2,1)}), bf16[32,32,1024]{2,1,0:T(8,128)(2,1)}, u32[]{:S(2)}, u32[]{:S(2)}) async-start(bf16[32,32,1024]{2,1,0:T(8,128)(2,1)} %scatter_fusion), calls=%async_computation.1 | async-start | bytes 4194304 | tf_op jit(solution)/shard_map/all_to_all | solution.py:84
  34.7 0.2 all-gather.9.cloned.1.call-start
  34.9 0.3 all-gather.9.cloned.1.call-update
  35.3 0.1 convert_reduce_fusion.2
  35.4 0.1 broadcast_in_dim.90
  35.5 0.1 reshape.200
  35.6 1.6 sort.17
  37.2 0.1 broadcast_in_dim.91
  37.2 0.1 broadcast_in_dim.92
  37.3 0.6 gather_fusion
  37.9 0.1 gather.13
  38.0 0.1 fusion.51
  38.1 0.1 compare_convert_fusion
  38.2 0.3 compare_and_fusion
  38.5 43.7 %all-to-all-done.1 = bf16[32,32,1024]{2,1,0:T(8,128)(2,1)} async-done(((bf16[32,32,1024]{2,1,0:T(8,128)(2,1)}), bf16[32,32,1024]{2,1,0:T(8,128)(2,1)}, u32[]{:S(2)}, u32[]{:S(2)}) %all-to-all-start.1) | async-done | bytes 2097184 | tf_op jit(solution)/shard_map/all_to_all | solution.py:84
  82.2 2.3 %gather_fusion.1 = bf16[32,32,1024]{2,1,0:T(8,128)(2,1)S(1)} fusion(bf16[32,32,1024]{2,1,0:T(8,128)(2,1)} %all-to-all-done.1, s32[1024]{0:T(1024)S(1)} %pad_clamp_fusion), kind=kCustom, calls=%fused_computation.1 | custom fusion | bytes 4194432 | tf_op jit(solution)/shard_map/jit(_take)/gather | solution.py:87
  84.5 0.5 convert_reduce_fusion
  85.1 0.1 div.23
  85.2 0.9 fusion.15
  86.0 0.1 rsqrt.20
  86.1 1.7 bitcast_select_fusion
  87.8 11.9 %convolution_convert_fusion = bf16[1024,3072]{1,0:T(8,128)(2,1)} fusion(bf16[1024,3072]{1,0:T(8,128)(2,1)} %all-gather.5.cloned.1.call-done, bf16[1024,1024]{1,0:T(8,128)(2,1)} %bitcast_select_fusion, f32[1024]{0:T(1024)S(1)} %rsqrt.20, f32[1024]{0:T(1024)S(1)} %div.23), kind=kOutput, calls=%fused_computation.19 | convolution fusion | flops 6449790976 | bytes 14688256 | tf_op jit(solution)/shard_map/dot_general | solution.py:92
  99.8 15.9 %reshape.201 = bf16[32,32,3,16,64]{4,3,2,1,0:T(8,128)(2,1)} reshape(bf16[1024,3072]{1,0:T(8,128)(2,1)} %convolution_convert_fusion) | data formatting | bytes 12582912 | tf_op jit(solution)/shard_map/reshape | solution.py:20
  115.7 7.3 %fusion.52 = (bf16[32,32,1,16,64]{4,3,2,1,0:T(8,128)(2,1)}, bf16[32,32,1,16,64]{4,3,2,1,0:T(8,128)(2,1)S(1)}, bf16[32,32,1,16,64]{4,3,2,1,0:T(8,128)(2,1)S(1)}) fusion(bf16[32,32,3,16,64]{4,3,2,1,0:T(8,128)(2,1)} %reshape.201), kind=kLoop, calls=%fused_computation.94 | loop fusion | bytes 12582912 | tf_op jit(solution)/shard_map/slice | solution.py:33
  123.0 2.3 %fusion.17 = f32[32,16,32,32]{2,3,1,0:T(8,128)S(1)} fusion(bf16[32,32,1,16,64]{4,3,2,1,0:T(8,128)(2,1)S(1)} %get-tuple-element.9, bf16[32,32,1,16,64]{4,3,2,1,0:T(8,128)(2,1)S(1)} %get-tuple-element.8), kind=kOutput, calls=%fused_computation.30 | convolution fusion | flops 67108864 | bytes 6291456 | tf_op jit(solution)/shard_map/nqhd,nkhd->nhqk/dot_general | solution.py:21
  125.3 5.1 %fusion.53 = (f32[32,16,32]{2,1,0:T(8,128)S(1)}, f32[32,16,32,32]{2,3,1,0:T(8,128)}) fusion(f32[32,16,32,32]{2,3,1,0:T(8,128)S(1)} %fusion.17, pred[32,32,32]{1,2,0:T(8,128)(4,1)S(1)} %compare_and_fusion), kind=kOutput, calls=%fused_computation.95 | output fusion | flops 3670047 | bytes 4292608 | tf_op jit(solution)/shard_map/sub | solution.py:28
  130.5 6.7 %convert_bitcast_fusion = bf16[32,32,16,64]{3,1,2,0:T(8,128)(2,1)S(1)} fusion(f32[32,16,32,32]{2,3,1,0:T(8,128)} %get-tuple-element.13, f32[32,16,32]{2,1,0:T(8,128)S(1)} %broadcast_add_fusion, bf16[32,32,1,16,64]{4,3,2,1,0:T(8,128)(2,1)} %get-tuple-element.7), kind=kOutput, calls=%fused_computation.36 | convolution fusion | flops 69206016 | bytes 6356992 | tf_op jit(solution)/shard_map/nhqk,nkhd->nqhd/dot_general | solution.py:32
  137.2 3.9 %copy.26 = bf16[32,32,16,64]{3,2,1,0:T(8,128)(2,1)} copy(bf16[32,32,16,64]{3,1,2,0:T(8,128)(2,1)S(1)} %convert_bitcast_fusion) | data formatting | bytes 4194304 | tf_op jit(solution)/shard_map/convert_element_type | solution.py:35
  141.1 5.5 %reshape.202 = bf16[1024,1024]{1,0:T(8,128)(2,1)S(1)} reshape(bf16[32,32,16,64]{3,2,1,0:T(8,128)(2,1)} %copy.26) | data formatting | bytes 4194304 | tf_op jit(solution)/shard_map/reshape | solution.py:35
  146.5 0.0 all-gather.7.cloned.1.call-done
  146.6 4.6 %fusion.54 = (f32[1024]{0:T(1024)S(1)}, f32[1024,1024]{1,0:T(8,128)S(1)}) fusion(bf16[1024,1024]{1,0:T(8,128)(2,1)S(1)} %reshape.202, bf16[1024,1024]{1,0:T(8,128)(2,1)} %all-gather.7.cloned.1.call-done, bf16[1024,1024]{1,0:T(8,128)(2,1)} %bitcast_select_fusion), kind=kOutput, calls=%fused_computation.96 | convolution fusion | flops 2150628352 | bytes 10489856 | tf_op jit(solution)/shard_map/dot_general | solution.py:94
  151.2 1.9 %copy-done = f32[1024,1024]{1,0:T(8,128)} copy-done((f32[1024,1024]{1,0:T(8,128)}, f32[1024,1024]{1,0:T(8,128)S(1)}, u32[]{:S(2)}) %copy-start) | copy-done | bytes 4194328
  153.1 0.6 multiply_reduce_fusion
  153.7 0.0 all-gather.11.cloned.1.call-done
  153.7 0.0 all-gather.9.cloned.1.call-done
  153.8 26.7 %select_convert_fusion = bf16[1024,1024]{1,0:T(8,128)(2,1)} fusion(f32[1024,1024]{1,0:T(8,128)} %copy-done, bf16[4096,1024]{1,0:T(8,128)(2,1)} %all-gather.11.cloned.1.call-done, bf16[1024,4096]{1,0:T(8,128)(2,1)} %all-gather.9.cloned.1.call-done, f32[1024]{0:T(1024)S(1)} %add_rsqrt_fusion.1, f32[1024]{0:T(1024)S(1)} %broadcast_multiply_fusion.1, ...), kind=kOutput, calls=%fused_computation.33 | convolution fusion | flops 17223909376 | bytes 23077888 | tf_op jit(solution)/shard_map/dot_general | solution.py:99
  (31 shorter events, 0.1 us)
Async XLA Ops:
  6.5 81.3 %all-gather.5.cloned.1.call-start = ((), (), s32[]{:S(2)}) async-start(), calls=%async_computation.2 | async-start | bytes 9437184 | tf_op jit(solution)/shard_map/all_gather | solution.py:46
  6.5 2.2 %copy-start.7 = (s32[1,16,32]{2,1,0:T(8,128)S(1)}, s32[1,16,32]{2,1,0:T(8,128)}, u32[]{:S(2)}) copy-start(s32[1,16,32]{2,1,0:T(8,128)} %param.17) | copy-start | bytes 6148
  6.5 2.4 %copy-start.5 = (s32[32,32]{1,0:T(8,128)S(1)}, s32[32,32]{1,0:T(8,128)}, u32[]{:S(2)}) copy-start(s32[32,32]{1,0:T(8,128)} %param.15) | copy-start | bytes 12292
  6.5 2.4 %copy-start.6 = (s32[32,32]{1,0:T(8,128)S(1)}, s32[32,32]{1,0:T(8,128)}, u32[]{:S(2)}) copy-start(s32[32,32]{1,0:T(8,128)} %param.16) | copy-start | bytes 12292
  6.5 10.8 %copy-start.3 = (s32[32,32]{1,0:T(8,128)S(1)}, s32[32,32]{1,0:T(8,128)}, u32[]{:S(2)}) copy-start(s32[32,32]{1,0:T(8,128)} %param.14) | copy-start | bytes 12292
  6.5 10.8 %copy-start.4 = (s32[32,32]{1,0:T(8,128)S(1)}, s32[32,32]{1,0:T(8,128)}, u32[]{:S(2)}) copy-start(s32[32,32]{1,0:T(8,128)} %param.13) | copy-start | bytes 12292
  6.6 11.2 %copy-start.1 = (bf16[64,1024]{1,0:T(8,128)(2,1)S(1)}, bf16[64,1024]{1,0:T(8,128)(2,1)}, u32[]{:S(2)}) copy-start(bf16[64,1024]{1,0:T(8,128)(2,1)} %param.19) | copy-start | bytes 393220
  6.6 11.2 %copy-start.2 = (bf16[64,1024]{1,0:T(8,128)(2,1)S(1)}, bf16[64,1024]{1,0:T(8,128)(2,1)}, u32[]{:S(2)}) copy-start(bf16[64,1024]{1,0:T(8,128)(2,1)} %param.18) | copy-start | bytes 393220
  7.3 139.3 %all-gather.7.cloned.1.call-start = ((), (), s32[]{:S(2)}) async-start(), calls=%async_computation.3 | async-start | bytes 3145728 | tf_op jit(solution)/shard_map/all_gather | solution.py:47
  8.0 145.7 %all-gather.11.cloned.1.call-start = ((), (), s32[]{:S(2)}) async-start(), calls=%async_computation.5 | async-start | bytes 12582912 | tf_op jit(solution)/shard_map/all_gather | solution.py:49
  10.2 17.6 %all-to-all-start = ((bf16[16,2,32]{2,1,0:T(2,128)(2,1)}), bf16[16,2,32]{2,1,0:T(2,128)(2,1)S(1)}, u32[]{:S(2)}, u32[]{:S(2)}) async-start(bf16[16,2,32]{2,1,0:T(2,128)(2,1)} %bitcast.4), calls=%async_computation | async-start | bytes 16384 | tf_op jit(solution)/shard_map/all_to_all | solution.py:85
  27.8 54.5 %all-to-all-start.1 = ((bf16[32,32,1024]{2,1,0:T(8,128)(2,1)}), bf16[32,32,1024]{2,1,0:T(8,128)(2,1)}, u32[]{:S(2)}, u32[]{:S(2)}) async-start(bf16[32,32,1024]{2,1,0:T(8,128)(2,1)} %scatter_fusion), calls=%async_computation.1 | async-start | bytes 4194304 | tf_op jit(solution)/shard_map/all_to_all | solution.py:84
  34.7 119.0 %all-gather.9.cloned.1.call-start = ((), (), s32[]{:S(2)}) async-start(), calls=%async_computation.4 | async-start | bytes 12582912 | tf_op jit(solution)/shard_map/all_gather | solution.py:48
  151.2 1.9 %copy-start = (f32[1024,1024]{1,0:T(8,128)}, f32[1024,1024]{1,0:T(8,128)S(1)}, u32[]{:S(2)}) copy-start(f32[1024,1024]{1,0:T(8,128)S(1)} %get-tuple-element.15) | copy-start | bytes 12582916
Sparse Core Ops, SparseCore 0:
  8.9 18.1 all-gather.4
  28.6 11.7 all-gather.6
  42.0 20.9 all-gather.10
  64.4 21.0 all-gather.8
where the time goes:
time: 188 us; the launch traced here: 187 us
  matrix products  55 us (29%)
  waiting for transfers between devices  46.1 us (25%)
  local copies, waits for them, and re-layouts  45.2 us (24%)
  starting transfers between devices  14.4 us (8%)
  between operations  13.4 us (7%)
  other arithmetic  12.9 us (7%)
    all_to_all x1, waiting for transfers between devices, local(): lax.all_to_all(outgoing, 'dp', split_axis=0, concat_axis=0, tiled=True)  43.7 us
    dot_general x1, matrix products, local(): lowered = jnp.dot(activated, full[3], preferred_element_type=jnp.float32)  26.7 us
    reshape x1, local copies, waits for them, and re-layouts, attend(): parts = qkv.reshape(count, seq, 3, HEADS, HEAD_DIM)  15.9 us
    dot_general x1, matrix products, local(): qkv = jnp.dot(normed, full[0], preferred_element_type=jnp.float32)  11.9 us
    slice x1, local copies, waits for them, and re-layouts, attend(): parts[:, :, 2]  7.29 us
    all_to_all x1, starting transfers between devices, local(): lax.all_to_all(outgoing_labels, 'dp', split_axis=0, concat_axis=0, tiled=...  7.17 us
    all_to_all x1, starting transfers between devices, local(): lax.all_to_all(outgoing, 'dp', split_axis=0, concat_axis=0, tiled=True)  6.9 us
    dot_general x1, matrix products, attend(): jnp.einsum('nhqk,nkhd->nqhd', probs, parts[:, :, 2], preferred_element_ty...  6.7 us
  transfers between devices with their start and end apart: 6, of which 1 were waited for; matrix products, arithmetic and copies ran while one was open for 45% of the time, Pallas kernels for 0%

commit v1 on v0

--- a/solution.py
+++ b/solution.py
@@ -1,6 +1,8 @@
 import jax
 import jax.numpy as jnp
 from jax import lax
+from jax.experimental import pallas as pl
+from jax.experimental.pallas import tpu as pltpu
 from jax.sharding import PartitionSpec as P
 
 HEADS = 16
@@ -102,6 +104,356 @@
     return jnp.where(live, result, 0.0).astype(jnp.bfloat16).reshape(count, seq, width)
 
 
+MESH = pl.DeviceIdType.MESH
+ROWS = 128
+BF16 = jnp.bfloat16
+F32 = jnp.float32
+
+
+def loop(count, step):
+    lax.fori_loop(0, count, lambda i, carry: (step(i), carry)[1], 0)
+
+
+def layer_kernel(
+    perm, onehot, lab, patches, row_table, col_table, w_qkv, w_out, w_up, w_down,
+    out,
+    pv, tab, wq, wo, wu, wd, x, sb, labs, lsend, normed, qkv, att, mid, alive, res,
+    local_sem, w_local, w_send, w_recv, b_send, b_recv, l_send, l_recv, a_send, a_recv,
+):
+    peers, seq, width = sb.shape
+    half = peers * seq
+    blocks = half // ROWS
+    per = ROWS // seq
+    heads = width // (2 * HEAD_DIM)
+    mlp = wu.shape[1]
+    grid = row_table.shape[0]
+    me = lax.axis_index("dp")
+    core = lax.axis_index("fsdp")
+    other = 1 - core
+
+    barrier = pltpu.get_barrier_semaphore()
+
+    def greet(step):
+        peer = lax.rem(me + step + 1, peers)
+        pl.semaphore_signal(barrier, inc=1, device_id={"dp": peer}, device_id_type=MESH)
+
+    pl.semaphore_signal(barrier, inc=1, device_id={"fsdp": other}, device_id_type=MESH)
+    loop(peers - 1, greet)
+
+    weights = ((w_qkv, wq), (w_out, wo), (w_up, wu), (w_down, wd))
+
+    def own(i):
+        src, dst = weights[i]
+        return pltpu.make_async_copy(
+            src, dst.at[pl.ds(core * src.shape[0], src.shape[0])], w_local.at[i]
+        )
+
+    def swap(i):
+        src, dst = weights[i]
+        return pltpu.make_async_remote_copy(
+            src_ref=src,
+            dst_ref=dst.at[pl.ds(core * src.shape[0], src.shape[0])],
+            send_sem=w_send.at[i],
+            recv_sem=w_recv.at[i],
+            device_id={"fsdp": other},
+            device_id_type=MESH,
+        )
+
+    first = (
+        pltpu.make_async_copy(patches, pv, local_sem.at[0]),
+        pltpu.make_async_copy(row_table, tab.at[pl.ds(0, grid)], local_sem.at[1]),
+        pltpu.make_async_copy(col_table, tab.at[pl.ds(grid, grid)], local_sem.at[2]),
+    )
+    for copy in first:
+        copy.start()
+    for i in range(4):
+        own(i).start()
+    for copy in first:
+        copy.wait()
+
+    def embed(slot):
+        at = perm[slot]
+        places = jnp.dot(onehot[at], tab[...], preferred_element_type=F32)
+        return (pv[at].astype(F32) + places).astype(BF16)
+
+    def embed_sent(r):
+        sb[r] = embed(2 * r + 1)
+        lsend[r] = lab[perm[2 * r + 1]]
+
+    loop(peers, embed_sent)
+
+    pl.semaphore_wait(barrier, peers)
+    swap(0).start()
+
+    def token_copy(step):
+        peer = lax.rem(me + step, peers)
+        return pltpu.make_async_remote_copy(
+            src_ref=sb.at[peer],
+            dst_ref=x.at[1, pl.ds(me * seq, seq)],
+            send_sem=b_send.at[step],
+            recv_sem=b_recv.at[step],
+            device_id={"dp": peer},
+            device_id_type=MESH,
+        )
+
+    def label_copy(step):
+        peer = lax.rem(me + step, peers)
+        return pltpu.make_async_remote_copy(
+            src_ref=lsend.at[peer],
+            dst_ref=labs.at[1, me],
+            send_sem=l_send.at[step],
+            recv_sem=l_recv.at[step],
+            device_id={"dp": peer},
+            device_id_type=MESH,
+        )
+
+    def send_tokens(i):
+        token_copy(i + 1).start()
+        label_copy(i + 1).start()
+
+    loop(peers - 1, send_tokens)
+    for i in range(1, 4):
+        swap(i).start()
+    keep_tokens = pltpu.make_async_copy(
+        sb.at[me], x.at[1, pl.ds(me * seq, seq)], local_sem.at[3]
+    )
+    keep_labels = pltpu.make_async_copy(lsend.at[me], labs.at[1, me], local_sem.at[4])
+    keep_tokens.start()
+    keep_labels.start()
+
+    def embed_kept(r):
+        x[0, pl.ds(pl.multiple_of(r * seq, seq), seq)] = embed(2 * r)
+        labs[0, r] = lab[perm[2 * r]]
+
+    loop(peers, embed_kept)
+
+    def result_copy(step):
+        peer = lax.rem(me + step, peers)
+        return pltpu.make_async_remote_copy(
+            src_ref=res.at[0, pl.ds(pl.multiple_of(peer * seq, seq), seq)],
+            dst_ref=out.at[me, 0],
+            send_sem=a_send.at[step],
+            recv_sem=a_recv.at[step],
+            device_id={"dp": peer},
+            device_id_type=MESH,
+        )
+
+    keep_result = pltpu.make_async_copy(
+        res.at[0, pl.ds(pl.multiple_of(me * seq, seq), seq)], out.at[me, 0], local_sem.at[5]
+    )
+
+    lane = lax.broadcasted_iota(jnp.int32, (1, ROWS), 1)
+    low = lane < HEAD_DIM
+    scale = HEAD_DIM ** (-0.5)
+    take_low = jnp.where(low, scale, 0.0).astype(BF16)
+    take_high = jnp.where(low, 0.0, scale).astype(BF16)
+    ones = jnp.ones((ROWS, ROWS), BF16)
+
+    def ready(h, i):
+        @pl.when(h == 0)
+        def _():
+            own(i).wait()
+            swap(i).wait_recv()
+
+    def run(h):
+        @pl.when(h == 1)
+        def _():
+            def arrive(i):
+                token_copy(i + 1).wait_recv()
+                label_copy(i + 1).wait_recv()
+
+            loop(peers - 1, arrive)
+            keep_tokens.wait()
+            keep_labels.wait()
+
+        def rows_of(i):
+            return pl.ds(pl.multiple_of(i * ROWS, ROWS), ROWS)
+
+        def norm_first(i):
+            rows = rows_of(i)
+            normed[rows] = layer_norm(x[h, rows].astype(F32)).astype(BF16)
+
+        loop(blocks, norm_first)
+        ready(h, 0)
+        tile = 512
+
+        def project(n):
+            cols = pl.ds(pl.multiple_of(n * tile, tile), tile)
+            qkv[:, cols] = jnp.dot(
+                normed[...], wq[:, cols], preferred_element_type=F32
+            ).astype(BF16)
+
+        loop(3 * width // tile, project)
+
+        def attend_block(i):
+            rows = rows_of(i)
+            label = jnp.zeros((8, ROWS), jnp.int32)
+            for q in range(per):
+                label = jnp.where(lane // seq == q, labs[h, i * per + q], label)
+            group = jnp.where(label > 0, label + 1024 * (lane // seq), 0).astype(F32)
+            row = jnp.broadcast_to(group[0:1], (ROWS, ROWS))
+            col = row.T
+            alive[rows] = col
+            bias = jnp.where((row == col) & (row > 0), 0.0, -1e30)
+            bias = jnp.concatenate([bias, bias], axis=0)
+
+            def pair(p):
+                def part(third):
+                    at = pl.multiple_of(third * width + p * ROWS, ROWS)
+                    return qkv[rows, pl.ds(at, ROWS)]
+
+                query = part(0)
+                query = jnp.concatenate([query * take_low, query * take_high], axis=0)
+                scores = bias + lax.dot_general(
+                    query, part(1), (((1,), (1,)), ((), ())), preferred_element_type=F32
+                )
+                peak = jnp.max(scores, axis=-1, keepdims=True)
+                probs = jnp.exp(scores - peak).astype(BF16)
+                value = jnp.concatenate([part(2), ones], axis=1)
+                mixed = jnp.dot(probs, value, preferred_element_type=F32)
+                mixed = jnp.where(low, mixed[:ROWS, :ROWS], mixed[ROWS:, :ROWS]) / jnp.where(
+                    low, mixed[:ROWS, ROWS:], mixed[ROWS:, ROWS:]
+                )
+                att[rows, pl.ds(pl.multiple_of(p * ROWS, ROWS), ROWS)] = mixed.astype(BF16)
+
+            def pairs(p):
+                for k in range(4):
+                    pair(4 * p + k)
+
+            loop(heads // 4, pairs)
+
+        loop(blocks, attend_block)
+        ready(h, 1)
+
+        def project_out(n):
+            cols = pl.ds(pl.multiple_of(n * tile, tile), tile)
+            mid[:, cols] = x[h, :, cols].astype(F32) + jnp.dot(
+                att[...], wo[:, cols], preferred_element_type=F32
+            )
+
+        loop(width // tile, project_out)
+
+        def norm_second(i):
+            rows = rows_of(i)
+            normed[rows] = layer_norm(mid[rows]).astype(BF16)
+
+        loop(blocks, norm_second)
+        ready(h, 2)
+        ready(h, 3)
+
+        def feed(c):
+            cols = pl.ds(pl.multiple_of(c * tile, tile), tile)
+            upper = jnp.dot(normed[...], wu[:, cols], preferred_element_type=F32)
+            active = jax.nn.gelu(upper, approximate=True).astype(BF16)
+            mid[...] += jnp.dot(active, wd[cols], preferred_element_type=F32)
+
+        loop(mlp // tile, feed)
+
+        def finish(i):
+            rows = rows_of(i)
+            res[h, rows] = jnp.where(alive[rows][:, 0:1] > 0, mid[rows], 0.0).astype(BF16)
+
+        loop(blocks, finish)
+
+        @pl.when(h == 0)
+        def _():
+            loop(peers - 1, lambda i: result_copy(i + 1).start())
+            keep_result.start()
+
+    loop(2, run)
+
+    def store(r):
+        return pltpu.make_async_copy(
+            res.at[1, pl.ds(pl.multiple_of(r * seq, seq), seq)], out.at[r, 1], b_recv.at[r]
+        )
+
+    loop(peers, lambda r: store(r).start())
+    keep_result.wait()
+
+    def drain(i):
+        token_copy(i + 1).wait_send()
+        label_copy(i + 1).wait_send()
+        result_copy(i + 1).wait()
+
+    loop(peers - 1, drain)
+    for i in range(4):
+        swap(i).wait_send()
+    loop(peers, lambda r: store(r).wait())
+
+
+def fused(
+    patches, rows, cols, keep, images, destination, row_table, col_table, w_qkv, w_out, w_up, w_down
+):
+    blk, seq, width = patches.shape
+    peers = lax.axis_size("dp")
+    grid = row_table.shape[0]
+    mlp = w_up.shape[1]
+    slots = jnp.arange(grid, dtype=jnp.int32)
+    onehot = jnp.concatenate(
+        [(rows[..., None] == slots).astype(BF16), (cols[..., None] == slots).astype(BF16)],
+        axis=-1,
+    )
+    labels = jnp.tile(keep * (images + 1), (1, ROWS // seq))
+    labels = jnp.broadcast_to(labels[:, None], (blk, 8, ROWS))
+    mine = lax.dynamic_index_in_dim(destination[0], lax.axis_index("dp"), 0, keepdims=False)
+    positions = jnp.arange(blk, dtype=jnp.int32)
+    ahead = (mine[:, None] > mine[None, :]) | (
+        (mine[:, None] == mine[None, :]) & (positions[:, None] > positions[None, :])
+    )
+    place = jnp.sum(ahead.astype(jnp.int32), axis=1)
+    perm = jnp.sum(jnp.where(place[None, :] == positions[:, None], positions[None, :], 0), axis=1)
+    half = peers * seq
+    anywhere = pl.BlockSpec(memory_space=pl.ANY)
+    vmem = pl.BlockSpec(memory_space=pltpu.VMEM)
+    dma = pltpu.SemaphoreType.DMA
+    out = pl.pallas_call(
+        layer_kernel,
+        out_shape=jax.ShapeDtypeStruct((peers, blk // peers, seq, width), BF16),
+        in_specs=[pl.BlockSpec(memory_space=pltpu.SMEM), vmem, vmem] + [anywhere] * 7,
+        out_specs=anywhere,
+        scratch_shapes=[
+            pltpu.VMEM((blk, seq, width), BF16),
+            pltpu.VMEM((2 * grid, width), BF16),
+            pltpu.VMEM((width, 3 * width), BF16),
+            pltpu.VMEM((width, width), BF16),
+            pltpu.VMEM((width, mlp), BF16),
+            pltpu.VMEM((mlp, width), BF16),
+            pltpu.VMEM((2, half, width), BF16),
+            pltpu.VMEM((peers, seq, width), BF16),
+            pltpu.VMEM((2, peers, 8, ROWS), jnp.int32),
+            pltpu.VMEM((peers, 8, ROWS), jnp.int32),
+            pltpu.VMEM((half, width), BF16),
+            pltpu.VMEM((half, 3 * width), BF16),
+            pltpu.VMEM((half, width), BF16),
+            pltpu.VMEM((half, width), F32),
+            pltpu.VMEM((half, ROWS), F32),
+            pltpu.VMEM((2, half, width), BF16),
+            dma((6,)),
+            dma((4,)),
+            dma((4,)),
+            dma((4,)),
+            dma((peers,)),
+            dma((peers,)),
+            dma((peers,)),
+            dma((peers,)),
+            dma((peers,)),
+            dma((peers,)),
+        ],
+        compiler_params=pltpu.CompilerParams(
+            collective_id=0, has_side_effects=True, vmem_limit_bytes=60 * 1024 * 1024
+        ),
+    )(perm, onehot, labels, patches, row_table, col_table, w_qkv, w_out, w_up, w_down)
+    return out.reshape(blk, seq, width)
+
+
+def choose(*args):
+    blk, seq, width = args[0].shape
+    peers = lax.axis_size("dp")
+    even = blk == 2 * peers and lax.axis_size("fsdp") == 2
+    fits = ROWS % seq == 0 and (peers * seq) % ROWS == 0 and width % 1024 == 0
+    return (fused if even and fits else local)(*args)
+
+
 def solution(mesh):
     in_specs = (
         P(("dp", "fsdp"), None, None),
@@ -118,4 +470,4 @@
         P("fsdp", None),
     )
     out_specs = P(("dp", "fsdp"), None, None)
-    return jax.shard_map(local, mesh=mesh, in_specs=in_specs, out_specs=out_specs, check_vma=False)
+    return jax.shard_map(choose, mesh=mesh, in_specs=in_specs, out_specs=out_specs, check_vma=False)

time: 188 us -> 77.9 us (0.41)
  Pallas kernels: 0 us -> 68.2 us
  matrix products: 55 us -> 0 us
  waiting for transfers between devices: 46.1 us -> 0 us
  local copies, waits for them, and re-layouts: 45.2 us -> 4.66 us
  starting transfers between devices: 14.4 us -> 0 us
  between operations: 13.4 us -> 0.02 us
  other arithmetic: 12.9 us -> 3.6 us
    pallas_call x0 -> x1, Pallas kernels: none -> 68.2 us  [fused(): pl.pallas_call(layer_kernel, out_shape=jax.ShapeDtypeStruct((peers, blk /...]
    dot_general x6 -> x0, matrix products: 55 us -> none  [the longest x1 26.7 us: local(): lowered = jnp.dot(activated, full[3], preferred_element_type=jnp.float32)]
    all_to_all x2 -> x0, waiting for transfers between devices: 43.7 us -> none  [the longest x1 43.7 us: local(): lax.all_to_all(outgoing, 'dp', split_axis=0, concat_axis=0, tiled=True)]
    reshape x3 -> x0, local copies, waits for them, and re-layouts: 21.5 us -> none  [the longest x1 15.9 us: attend(): parts = qkv.reshape(count, seq, 3, HEADS, HEAD_DIM)]
    all_to_all x2 -> x0, starting transfers between devices: 14.1 us -> none  [the longest x1 7.17 us: local(): lax.all_to_all(outgoing_labels, 'dp', split_axis=0, concat_axis=0, tiled=...]
    slice x1 -> x0, local copies, waits for them, and re-layouts: 7.29 us -> none  [attend(): parts[:, :, 2]]
    scatter x1 -> x0, local copies, waits for them, and re-layouts: 5.71 us -> none  [local(): jnp.zeros((peers * capacity, seq, width), jnp.bfloat16).at[sending_slot]]
    sub x1 -> x0, other arithmetic: 5.14 us -> none  [attend(): weights = jnp.where(allowed, jnp.exp(scores - peak), 0.0)]
  transfers between devices with their start and end apart: 6 -> 0, of which waited for: 1 -> 0; matrix products, arithmetic and copies ran while one was open for 45% -> 0% of each run, Pallas kernels for 0% -> 0%
where the time goes in v1:
time: 77.9 us; the launch traced here: 76.5 us
  Pallas kernels  68.2 us (88%)
  local copies, waits for them, and re-layouts  4.66 us (6%)
  other arithmetic  3.6 us (5%)
    pallas_call x1, Pallas kernels, fused(): pl.pallas_call(layer_kernel, out_shape=jax.ShapeDtypeStruct((peers, blk /...  68.2 us
    unnamed x3, local copies, waits for them, and re-layouts  3.88 us

profile of v1, /device:TPU:12, one launch (start us, length us, event | category | flops | bytes accessed | tf_op | source)
XLA Modules:
  0.0 76.5 jit_solution(16794281922876428583)
XLA Ops:
  0.0 0.0 copy-start
  0.0 0.7 copy-done
  0.7 0.2 convert_reduce_fusion
  0.9 0.7 select_reduce_fusion.perm
  1.6 0.7 add_multiply_fusion
  2.3 0.1 tile.9
  2.4 0.7 broadcast_in_dim.9.lab
  3.1 1.1 %iota_compare_fusion = (pred[32,32,64]{2,1,0:T(8,128)(4,1)S(1)}, pred[32,32,64]{2,1,0:T(8,128)(4,1)S(1)}) fusion(s32[32,32]{1,0:T(8,128)} %param.14, s32[32,32]{1,0:T(8,128)} %param.13), kind=kLoop, calls=%fused_computation | loop fusion | flops 131072 | bytes 139264 | tf_op jit(solution)/shard_map/eq | solution.py:393
  4.2 0.9 %add_convert_fusion.onehot = bf16[32,32,128]{2,1,0:T(8,128)(2,1)} fusion(pred[32,32,64]{2,1,0:T(8,128)(4,1)S(1)} %get-tuple-element.5, pred[32,32,64]{2,1,0:T(8,128)(4,1)S(1)} %get-tuple-element.6), kind=kLoop, calls=%fused_computation.2 | loop fusion | flops 262144 | bytes 393216 | tf_op jit(solution)/shard_map/concatenate | solution.py:392
  5.1 68.2 %shard_map.118 = bf16[16,2,32,1024]{3,2,1,0:T(8,128)(2,1)} custom-call(s32[32]{0:T(128)} %select_reduce_fusion.perm, bf16[32,32,128]{2,1,0:T(8,128)(2,1)} %add_convert_fusion.onehot, s32[32,8,128]{2,1,0:T(8,128)} %broadcast_in_dim.9.lab, bf16[32,32,1024]{2,1,0:T(8,128)(2,1)} %patches.1, bf16[64,1024]{1,0:T(8,128)(2,1)} %row_table.1, ...), custom_call_target="tpu_custom_call" | custom-call | tf_op jit(solution)/shard_map/pallas_call | solution.py:409
  73.4 3.2 %copy.14 = bf16[32,32,1024]{2,1,0:T(8,128)(2,1)} copy(bf16[32,32,1024]{2,1,0:T(8,128)(2,1)} %bitcast.3) | data formatting | bytes 4194304
  (2 shorter events, 0.0 us)
Async XLA Ops:
  0.0 0.7 copy-start

commit v2 on v1

--- a/solution.py
+++ b/solution.py
@@ -115,9 +115,9 @@
 
 
 def layer_kernel(
-    perm, onehot, lab, patches, row_table, col_table, w_qkv, w_out, w_up, w_down,
+    perm, rows_in, cols_in, keep_in, images_in, patches, row_table, col_table, w_qkv, w_out, w_up, w_down,
     out,
-    pv, tab, wq, wo, wu, wd, x, sb, labs, lsend, normed, qkv, att, mid, alive, res,
+    rows, cols, keep, images, pv, tab, wq, wo, wu, wd, x, sb, labs, lsend, normed, qkv, att, mid, alive, res,
     local_sem, w_local, w_send, w_recv, b_send, b_recv, l_send, l_recv, a_send, a_recv,
 ):
     peers, seq, width = sb.shape
@@ -148,13 +148,27 @@
             src, dst.at[pl.ds(core * src.shape[0], src.shape[0])], w_local.at[i]
         )
 
+    tile = 512
+    pieces = 3 * width // tile
+
     def swap(i):
         src, dst = weights[i]
         return pltpu.make_async_remote_copy(
             src_ref=src,
             dst_ref=dst.at[pl.ds(core * src.shape[0], src.shape[0])],
-            send_sem=w_send.at[i],
-            recv_sem=w_recv.at[i],
+            send_sem=w_send.at[pieces + i],
+            recv_sem=w_recv.at[pieces + i],
+            device_id={"fsdp": other},
+            device_id_type=MESH,
+        )
+
+    def swap_piece(n):
+        cols = pl.ds(pl.multiple_of(n * tile, tile), tile)
+        return pltpu.make_async_remote_copy(
+            src_ref=w_qkv.at[:, cols],
+            dst_ref=wq.at[pl.ds(core * w_qkv.shape[0], w_qkv.shape[0]), cols],
+            send_sem=w_send.at[n],
+            recv_sem=w_recv.at[n],
             device_id={"fsdp": other},
             device_id_type=MESH,
         )
@@ -163,6 +177,10 @@
         pltpu.make_async_copy(patches, pv, local_sem.at[0]),
         pltpu.make_async_copy(row_table, tab.at[pl.ds(0, grid)], local_sem.at[1]),
         pltpu.make_async_copy(col_table, tab.at[pl.ds(grid, grid)], local_sem.at[2]),
+        pltpu.make_async_copy(rows_in, rows, local_sem.at[6]),
+        pltpu.make_async_copy(cols_in, cols, local_sem.at[7]),
+        pltpu.make_async_copy(keep_in, keep, local_sem.at[8]),
+        pltpu.make_async_copy(images_in, images, local_sem.at[9]),
     )
     for copy in first:
         copy.start()
@@ -171,19 +189,30 @@
     for copy in first:
         copy.wait()
 
-    def embed(slot):
-        at = perm[slot]
-        places = jnp.dot(onehot[at], tab[...], preferred_element_type=F32)
-        return (pv[at].astype(F32) + places).astype(BF16)
-
-    def embed_sent(r):
-        sb[r] = embed(2 * r + 1)
-        lsend[r] = lab[perm[2 * r + 1]]
-
-    loop(peers, embed_sent)
+    def embed(i, which, target, tags):
+        at = [perm[2 * (i * per + q) + which] for q in range(per)]
+        row = jnp.concatenate([rows[pl.ds(a, 1)] for a in at], axis=1)
+        col = jnp.concatenate([cols[pl.ds(a, 1)] for a in at], axis=1)
+        spot = lax.broadcasted_iota(jnp.int32, (ROWS, ROWS), 0)
+        hot = jnp.where(spot < grid, row, col + grid) == spot
+        hot = jnp.where(hot, 1.0, 0.0).T.astype(BF16)
+        places = jnp.dot(hot, tab[...], preferred_element_type=F32)
+        for q in range(per):
+            place = places[q * seq:(q + 1) * seq]
+            target(i * per + q, (pv[at[q]].astype(F32) + place).astype(BF16))
+            tag = keep[pl.ds(at[q], 1)] * (images[pl.ds(at[q], 1)] + 1)
+            tags[i * per + q] = jnp.broadcast_to(jnp.concatenate([tag] * per, axis=1), (8, ROWS))
+
+    def set_sent(r, value):
+        sb[r] = value
+
+    def set_kept(r, value):
+        x[0, pl.ds(pl.multiple_of(r * seq, seq), seq)] = value
+
+    loop(blocks, lambda i: embed(i, 1, set_sent, lsend))
 
     pl.semaphore_wait(barrier, peers)
-    swap(0).start()
+    loop(pieces, lambda n: swap_piece(n).start())
 
     def token_copy(step):
         peer = lax.rem(me + step, peers)
@@ -221,11 +250,7 @@
     keep_tokens.start()
     keep_labels.start()
 
-    def embed_kept(r):
-        x[0, pl.ds(pl.multiple_of(r * seq, seq), seq)] = embed(2 * r)
-        labs[0, r] = lab[perm[2 * r]]
-
-    loop(peers, embed_kept)
+    loop(blocks, lambda i: embed(i, 0, set_kept, labs.at[0]))
 
     def result_copy(step):
         peer = lax.rem(me + step, peers)
@@ -255,6 +280,11 @@
             own(i).wait()
             swap(i).wait_recv()
 
+    def ready_own(h, i):
+        @pl.when(h == 0)
+        def _():
+            own(i).wait()
+
     def run(h):
         @pl.when(h == 1)
         def _():
@@ -274,16 +304,19 @@
             normed[rows] = layer_norm(x[h, rows].astype(F32)).astype(BF16)
 
         loop(blocks, norm_first)
-        ready(h, 0)
-        tile = 512
+        ready_own(h, 0)
 
         def project(n):
+            @pl.when(h == 0)
+            def _():
+                swap_piece(n).wait_recv()
+
             cols = pl.ds(pl.multiple_of(n * tile, tile), tile)
             qkv[:, cols] = jnp.dot(
                 normed[...], wq[:, cols], preferred_element_type=F32
             ).astype(BF16)
 
-        loop(3 * width // tile, project)
+        loop(pieces, project)
 
         def attend_block(i):
             rows = rows_of(i)
@@ -317,10 +350,10 @@
                 att[rows, pl.ds(pl.multiple_of(p * ROWS, ROWS), ROWS)] = mixed.astype(BF16)
 
             def pairs(p):
-                for k in range(4):
-                    pair(4 * p + k)
-
-            loop(heads // 4, pairs)
+                for k in range(8):
+                    pair(8 * p + k)
+
+            loop(heads // 8, pairs)
 
         loop(blocks, attend_block)
         ready(h, 1)
@@ -339,15 +372,22 @@
 
         loop(blocks, norm_second)
         ready(h, 2)
-        ready(h, 3)
-
-        def feed(c):
-            cols = pl.ds(pl.multiple_of(c * tile, tile), tile)
+        ready_own(h, 3)
+        wide = 1024
+        steps = mlp // wide
+
+        def feed(step):
+            @pl.when((h == 0) & (step == steps // 2))
+            def _():
+                swap(3).wait_recv()
+
+            c = lax.rem(step + core * (steps // 2), steps)
+            cols = pl.ds(pl.multiple_of(c * wide, wide), wide)
             upper = jnp.dot(normed[...], wu[:, cols], preferred_element_type=F32)
             active = jax.nn.gelu(upper, approximate=True).astype(BF16)
             mid[...] += jnp.dot(active, wd[cols], preferred_element_type=F32)
 
-        loop(mlp // tile, feed)
+        loop(steps, feed)
 
         def finish(i):
             rows = rows_of(i)
@@ -376,7 +416,8 @@
         result_copy(i + 1).wait()
 
     loop(peers - 1, drain)
-    for i in range(4):
+    loop(pieces, lambda n: swap_piece(n).wait_send())
+    for i in range(1, 4):
         swap(i).wait_send()
     loop(peers, lambda r: store(r).wait())
 
@@ -388,13 +429,6 @@
     peers = lax.axis_size("dp")
     grid = row_table.shape[0]
     mlp = w_up.shape[1]
-    slots = jnp.arange(grid, dtype=jnp.int32)
-    onehot = jnp.concatenate(
-        [(rows[..., None] == slots).astype(BF16), (cols[..., None] == slots).astype(BF16)],
-        axis=-1,
-    )
-    labels = jnp.tile(keep * (images + 1), (1, ROWS // seq))
-    labels = jnp.broadcast_to(labels[:, None], (blk, 8, ROWS))
     mine = lax.dynamic_index_in_dim(destination[0], lax.axis_index("dp"), 0, keepdims=False)
     positions = jnp.arange(blk, dtype=jnp.int32)
     ahead = (mine[:, None] > mine[None, :]) | (
@@ -404,14 +438,18 @@
     perm = jnp.sum(jnp.where(place[None, :] == positions[:, None], positions[None, :], 0), axis=1)
     half = peers * seq
     anywhere = pl.BlockSpec(memory_space=pl.ANY)
-    vmem = pl.BlockSpec(memory_space=pltpu.VMEM)
+    hbm = pl.BlockSpec(memory_space=pltpu.HBM)
     dma = pltpu.SemaphoreType.DMA
     out = pl.pallas_call(
         layer_kernel,
         out_shape=jax.ShapeDtypeStruct((peers, blk // peers, seq, width), BF16),
-        in_specs=[pl.BlockSpec(memory_space=pltpu.SMEM), vmem, vmem] + [anywhere] * 7,
+        in_specs=[pl.BlockSpec(memory_space=pltpu.SMEM)] + [hbm] * 11,
         out_specs=anywhere,
         scratch_shapes=[
+            pltpu.VMEM((blk, seq), jnp.int32),
+            pltpu.VMEM((blk, seq), jnp.int32),
+            pltpu.VMEM((blk, seq), jnp.int32),
+            pltpu.VMEM((blk, seq), jnp.int32),
             pltpu.VMEM((blk, seq, width), BF16),
             pltpu.VMEM((2 * grid, width), BF16),
             pltpu.VMEM((width, 3 * width), BF16),
@@ -428,10 +466,10 @@
             pltpu.VMEM((half, width), F32),
             pltpu.VMEM((half, ROWS), F32),
             pltpu.VMEM((2, half, width), BF16),
-            dma((6,)),
+            dma((10,)),
             dma((4,)),
-            dma((4,)),
-            dma((4,)),
+            dma((3 * width // 512 + 4,)),
+            dma((3 * width // 512 + 4,)),
             dma((peers,)),
             dma((peers,)),
             dma((peers,)),
@@ -442,7 +480,7 @@
         compiler_params=pltpu.CompilerParams(
             collective_id=0, has_side_effects=True, vmem_limit_bytes=60 * 1024 * 1024
         ),
-    )(perm, onehot, labels, patches, row_table, col_table, w_qkv, w_out, w_up, w_down)
+    )(perm, rows, cols, keep, images, patches, row_table, col_table, w_qkv, w_out, w_up, w_down)
     return out.reshape(blk, seq, width)
 
 
@@ -450,7 +488,7 @@
     blk, seq, width = args[0].shape
     peers = lax.axis_size("dp")
     even = blk == 2 * peers and lax.axis_size("fsdp") == 2
-    fits = ROWS % seq == 0 and (peers * seq) % ROWS == 0 and width % 1024 == 0
+    fits = 2 * args[6].shape[0] == ROWS and ROWS % seq == 0 and (peers * seq) % ROWS == 0 and width % 1024 == 0
     return (fused if even and fits else local)(*args)
 
 

time: 77.9 us -> 64.2 us (0.82); the launches traced: 76.5 us -> 63.8 us
  Pallas kernels: 68.2 us -> 59.1 us
  other arithmetic: 3.6 us -> 0.82 us
    pallas_call x1, Pallas kernels: 68.2 us -> 59.1 us  [fused(): pl.pallas_call(layer_kernel, out_shape=jax.ShapeDtypeStruct((peers, blk /...]
    eq x1 -> x0, other arithmetic: 1.07 us -> none  [fused(): cols[..., None] == slots]
    concatenate x1 -> x0, other arithmetic: 0.91 us -> none  [fused(): jnp.concatenate([(rows[..., None] == slots).astype(BF16), (cols[..., None...]
where the time goes in v2:
time: 64.2 us; the launch traced here: 63.8 us
  Pallas kernels  59.1 us (92%)
  local copies, waits for them, and re-layouts  3.89 us (6%)
  other arithmetic  0.82 us (1%)
    pallas_call x1, Pallas kernels, fused(): pl.pallas_call(layer_kernel, out_shape=jax.ShapeDtypeStruct((peers, blk /...  59.1 us
    unnamed x3, local copies, waits for them, and re-layouts  3.88 us

profile of v2, /device:TPU:12, one launch (start us, length us, event | category | flops | bytes accessed | tf_op | source)
XLA Modules:
  0.0 63.8 jit_solution(11914103969160265145)
XLA Ops:
  0.0 0.0 copy-start
  0.0 0.7 %copy-done = s32[1,16,32]{2,1,0:T(8,128)S(1)} copy-done((s32[1,16,32]{2,1,0:T(8,128)S(1)}, s32[1,16,32]{2,1,0:T(8,128)}, u32[]{:S(2)}) %copy-start) | copy-done | bytes 2072
  0.7 0.2 convert_reduce_fusion
  0.9 0.6 select_reduce_fusion.perm
  1.5 59.1 %shard_map.118 = bf16[16,2,32,1024]{3,2,1,0:T(8,128)(2,1)} custom-call(s32[32]{0:T(128)} %select_reduce_fusion.perm, s32[32,32]{1,0:T(8,128)} %rows_in.1, s32[32,32]{1,0:T(8,128)} %cols_in.1, s32[32,32]{1,0:T(8,128)} %keep_in.1, s32[32,32]{1,0:T(8,128)} %images_in.1, bf16[32,32,1024]{2,1,0:T(8,128)(2,1)} %patches.1, bf16[64,1024]{1,0:T(8,128)(2,1)} %row_table.1, ...), custom_call_target="tpu_custom_call" | custom-call | tf_op jit(solution)/shard_map/pallas_call | solution.py:443
  60.6 3.2 %copy.14 = bf16[32,32,1024]{2,1,0:T(8,128)(2,1)} copy(bf16[32,32,1024]{2,1,0:T(8,128)(2,1)} %bitcast.3) | data formatting | bytes 4194304
  (1 shorter events, 0.0 us)
Async XLA Ops:
  0.0 0.7 %copy-start = (s32[1,16,32]{2,1,0:T(8,128)S(1)}, s32[1,16,32]{2,1,0:T(8,128)}, u32[]{:S(2)}) copy-start(s32[1,16,32]{2,1,0:T(8,128)} %param.17) | copy-start | bytes 6148
